TPU v7x, 32 devices: a whole 2x2x4 slice. The times are simulated.
32 devices in a mesh: dp: 16 (over z, y, x), seq: 2 (over core).
Axes of the slice: x: 2, y: 2, z: 4, core: 2. Of those that a mesh axis runs over, the one named last changes fastest.
Arguments:
- tokens: bfloat16 [32, 512, 768], P('dp', 'seq'), may hold values from -6 to 6
- lengths: int32 [32], P('dp'), may hold values from 128 to 512, as said below
- cotangent: bfloat16 [32, 512, 768], P('dp', 'seq'), may hold values from -6 to 6
- w_query: bfloat16 [768, 768], P(('dp', 'seq')), may hold values from -0.3125 to 0.3125
- b_query: bfloat16 [768], P(('dp', 'seq')), may hold values from -3 to 3
- w_key: bfloat16 [768, 768], P(('dp', 'seq')), may hold values from -0.21875 to 0.21875
- w_value: bfloat16 [768, 768], P(('dp', 'seq')), may hold values from -0.21875 to 0.21875
- b_value: bfloat16 [768], P(('dp', 'seq')), may hold values from -3 to 3
- w_out: bfloat16 [768, 768], P(('dp', 'seq')), may hold values from -1.5 to 1.5
- b_out: bfloat16 [768], P(('dp', 'seq')), may hold values from -3 to 3
- gain_one: bfloat16 [768], P(('dp', 'seq')), may hold values from 0.25 to 1.75
- shift_one: bfloat16 [768], P(('dp', 'seq')), may hold values from -3 to 3
- w_inner: bfloat16 [768, 3072], P(('dp', 'seq')), may hold values from -0.21875 to 0.21875
- b_inner: bfloat16 [3072], P(('dp', 'seq')), may hold values from -3 to 3
- w_outer: bfloat16 [3072, 768], P(('dp', 'seq')), may hold values from -0.15625 to 0.15625
- b_outer: bfloat16 [768], P(('dp', 'seq')), may hold values from -3 to 3
- gain_two: bfloat16 [768], P(('dp', 'seq')), may hold values from 0.25 to 1.75
- shift_two: bfloat16 [768], P(('dp', 'seq')), may hold values from -3 to 3
Outputs:
- output: float32 [32, 512, 768], P('dp', 'seq')
- grad_tokens: float32 [32, 512, 768], P('dp', 'seq')
- grad_w_query: float32 [768, 768], P(('dp', 'seq'))
- grad_b_query: float32 [768], P(('dp', 'seq'))
- grad_w_key: float32 [768, 768], P(('dp', 'seq'))
- grad_w_value: float32 [768, 768], P(('dp', 'seq'))
- grad_b_value: float32 [768], P(('dp', 'seq'))
- grad_w_out: float32 [768, 768], P(('dp', 'seq'))
- grad_b_out: float32 [768], P(('dp', 'seq'))
- grad_gain_one: float32 [768], P(('dp', 'seq'))
- grad_shift_one: float32 [768], P(('dp', 'seq'))
- grad_w_inner: float32 [768, 3072], P(('dp', 'seq'))
- grad_b_inner: float32 [3072], P(('dp', 'seq'))
- grad_w_outer: float32 [3072, 768], P(('dp', 'seq'))
- grad_b_outer: float32 [768], P(('dp', 'seq'))
- grad_gain_two: float32 [768], P(('dp', 'seq'))
- grad_shift_two: float32 [768], P(('dp', 'seq'))
Inputs may be any that keep to these rules, and one draw needn't show every extreme that they name: lengths[s] counts the valid leading positions of sequence s; in every draw some sequence has exactly 512 and some exactly 128.
All inputs are finite; a program needn't handle non-finite values.
Results may differ from a plain program's by a relative error of at most 0.015.
Values may be sent and summed in bfloat16 or wider, within the bound.
No kernel may reach another device: no remote copies, remote signals or barrier semaphores. Data moves between devices by JAX's collectives and lax.ppermute only.
A program may use at most 192 MiB of HBM per device.

v0:
```python
import jax
import jax.numpy as jnp
from jax import lax
from jax.sharding import PartitionSpec as P

HEAD_DIM = 64
MB = 2


NEG_BIG = -1000000000.0
EPSILON = 1e-05
ROOT_HALF = 0.7071067811865476
INV_ROOT_TAU = 0.3989422804014327


def product(left, right):
    return jnp.dot(left, right, preferred_element_type=jnp.float32)


def product_tn(left, right):
    return lax.dot_general(
        left, right, (((0,), (0,)), ((), ())), preferred_element_type=jnp.float32
    )


def product_nt(left, right):
    return lax.dot_general(
        left, right, (((1,), (1,)), ((), ())), preferred_element_type=jnp.float32
    )


def column_sum(values):
    return jnp.sum(values, axis=0, dtype=jnp.float32)


def gelu_exact(values):
    return 0.5 * values * (1.0 + jax.scipy.special.erf(values * ROOT_HALF))


def gelu_slope(values):
    cumulative = 0.5 * (1.0 + jax.scipy.special.erf(values * ROOT_HALF))
    return cumulative + values * jnp.exp(-0.5 * values * values) * INV_ROOT_TAU


def normalize_keep(values, gain, shift):
    center = values - jnp.mean(values, axis=-1, keepdims=True)
    inv_spread = lax.rsqrt(jnp.mean(center * center, axis=-1, keepdims=True) + EPSILON)
    normed = center * inv_spread
    return (normed * gain + shift, normed, inv_spread)


def normalize_back(grad_out, normed, inv_spread, gain):
    grad_normed = grad_out * gain
    centered = grad_normed - jnp.mean(grad_normed, axis=-1, keepdims=True)
    grad_in = inv_spread * (
        centered - normed * jnp.mean(grad_normed * normed, axis=-1, keepdims=True)
    )
    return (grad_in, jnp.sum(grad_out * normed, axis=0), jnp.sum(grad_out, axis=0))


def split_heads(values):
    count, length, width = values.shape
    return values.reshape(count, length, width // HEAD_DIM, HEAD_DIM)


def score_table(queries, keys_all, visible):
    raw = jnp.einsum(
        "bqhd,bkhd->bhqk",
        split_heads(queries),
        split_heads(keys_all),
        preferred_element_type=jnp.float32,
    )
    return jnp.where(visible, raw * HEAD_DIM ** (-0.5), NEG_BIG)


def unpack(gathered):
    return tuple((piece if piece.ndim == 2 else piece.astype(jnp.float32) for piece in gathered))


def body(
    tokens,
    lengths,
    cotangent,
    w_query,
    b_query,
    w_key,
    w_value,
    b_value,
    w_out,
    b_out,
    gain_one,
    shift_one,
    w_inner,
    b_inner,
    w_outer,
    b_outer,
    gain_two,
    shift_two,
):
    shards = (
        w_query,
        b_query,
        w_key,
        w_value,
        b_value,
        w_out,
        b_out,
        gain_one,
        shift_one,
        w_inner,
        b_inner,
        w_outer,
        b_outer,
        gain_two,
        shift_two,
    )
    seq_count, half, width = tokens.shape
    group = seq_count // MB
    scale = HEAD_DIM ** (-0.5)
    seq_devices = lax.axis_size("seq")
    full_len = half * seq_devices
    totals = tuple((jnp.zeros(piece.shape, jnp.float32) for piece in shards))
    outputs = []
    input_grads = []
    positions_all = jnp.arange(full_len, dtype=jnp.int32)
    positions_local = lax.axis_index("seq") * half + jnp.arange(half, dtype=jnp.int32)
    for index in range(MB):
        first_seq = index * group
        tok_blk = tokens[first_seq : first_seq + group]
        cot_blk = cotangent[first_seq : first_seq + group]
        seq_lengths = lengths[first_seq : first_seq + group]
        rows = group * half
        gathered = (
            lax.all_gather(shards[0], ("dp", "seq"), axis=0, tiled=True),
            lax.all_gather(shards[1], ("dp", "seq"), axis=0, tiled=True),
            lax.all_gather(shards[2], ("dp", "seq"), axis=0, tiled=True),
            lax.all_gather(shards[3], ("dp", "seq"), axis=0, tiled=True),
            lax.all_gather(shards[4], ("dp", "seq"), axis=0, tiled=True),
            lax.all_gather(shards[5], ("dp", "seq"), axis=0, tiled=True),
            lax.all_gather(shards[6], ("dp", "seq"), axis=0, tiled=True),
            lax.all_gather(shards[7], ("dp", "seq"), axis=0, tiled=True),
            lax.all_gather(shards[8], ("dp", "seq"), axis=0, tiled=True),
            lax.all_gather(shards[9], ("dp", "seq"), axis=0, tiled=True),
            lax.all_gather(shards[10], ("dp", "seq"), axis=0, tiled=True),
            lax.all_gather(shards[11], ("dp", "seq"), axis=0, tiled=True),
            lax.all_gather(shards[12], ("dp", "seq"), axis=0, tiled=True),
            lax.all_gather(shards[13], ("dp", "seq"), axis=0, tiled=True),
            lax.all_gather(shards[14], ("dp", "seq"), axis=0, tiled=True),
        )
        (
            all_query,
            bias_query,
            all_key,
            all_value,
            bias_value,
            all_out,
            bias_out,
            gain_a,
            shift_a,
            all_inner,
            bias_inner,
            all_outer,
            bias_outer,
            gain_b,
            shift_b,
        ) = unpack(gathered)
        tok_rows = tok_blk.reshape(rows, width)
        queries = (
            (product(tok_rows, all_query) + bias_query)
            .astype(jnp.bfloat16)
            .reshape(group, half, width)
        )
        keys_here = product(tok_rows, all_key).astype(jnp.bfloat16).reshape(group, half, width)
        values_here = (
            (product(tok_rows, all_value) + bias_value)
            .astype(jnp.bfloat16)
            .reshape(group, half, width)
        )
        keys_all, values_all = (
            lax.all_gather(keys_here, "seq", axis=1, tiled=True),
            lax.all_gather(values_here, "seq", axis=1, tiled=True),
        )
        att_len = queries.shape[1]
        att_width = queries.shape[2]
        visible = (positions_all[None, :] < seq_lengths[:, None])[:, None, None, :]
        masked = score_table(queries, keys_all, visible)
        top = jnp.max(masked, axis=-1, keepdims=True)
        weights = jnp.exp(masked - top)
        total = jnp.sum(weights, axis=-1, keepdims=True)
        log_total = top + jnp.log(total)
        probs_low = (weights / total).astype(jnp.bfloat16)
        context = jnp.einsum(
            "bhqk,bkhd->bqhd",
            probs_low,
            split_heads(values_all),
            preferred_element_type=jnp.float32,
        )
        context = context.reshape(group, att_len, att_width).astype(jnp.bfloat16)
        context = context.reshape(rows, width)
        attn_out = product(context, all_out) + bias_out
        hidden, normed_one, inv_one = normalize_keep(
            tok_rows.astype(jnp.float32) + attn_out, gain_a, shift_a
        )
        hidden_low = hidden.astype(jnp.bfloat16)
        inner = product(hidden_low, all_inner) + bias_inner
        active = gelu_exact(inner).astype(jnp.bfloat16)
        outer = product(active, all_outer) + bias_outer
        output, normed_two, inv_two = normalize_keep(hidden + outer, gain_b, shift_b)
        gathered = (
            lax.all_gather(shards[0], ("dp", "seq"), axis=0, tiled=True),
            lax.all_gather(shards[1], ("dp", "seq"), axis=0, tiled=True),
            lax.all_gather(shards[2], ("dp", "seq"), axis=0, tiled=True),
            lax.all_gather(shards[3], ("dp", "seq"), axis=0, tiled=True),
            lax.all_gather(shards[4], ("dp", "seq"), axis=0, tiled=True),
            lax.all_gather(shards[5], ("dp", "seq"), axis=0, tiled=True),
            lax.all_gather(shards[6], ("dp", "seq"), axis=0, tiled=True),
            lax.all_gather(shards[7], ("dp", "seq"), axis=0, tiled=True),
            lax.all_gather(shards[8], ("dp", "seq"), axis=0, tiled=True),
            lax.all_gather(shards[9], ("dp", "seq"), axis=0, tiled=True),
            lax.all_gather(shards[10], ("dp", "seq"), axis=0, tiled=True),
            lax.all_gather(shards[11], ("dp", "seq"), axis=0, tiled=True),
            lax.all_gather(shards[12], ("dp", "seq"), axis=0, tiled=True),
            lax.all_gather(shards[13], ("dp", "seq"), axis=0, tiled=True),
            lax.all_gather(shards[14], ("dp", "seq"), axis=0, tiled=True),
        )
        (
            all_query,
            bias_query,
            all_key,
            all_value,
            bias_value,
            all_out,
            bias_out,
            gain_a,
            shift_a,
            all_inner,
            bias_inner,
            all_outer,
            bias_outer,
            gain_b,
            shift_b,
        ) = unpack(gathered)
        live = (
            (positions_local[None, :] < seq_lengths[:, None]).astype(jnp.float32).reshape(rows, 1)
        )
        grad_y = cot_blk.reshape(rows, width).astype(jnp.float32) * live
        grad_resid_two, grad_gain_two, grad_shift_two = normalize_back(
            grad_y, normed_two, inv_two, gain_b
        )
        grad_outer = grad_resid_two.astype(jnp.bfloat16)
        grad_b_outer = column_sum(grad_outer)
        grad_w_outer = product_tn(active, grad_outer)
        grad_inner = (product_nt(grad_outer, all_outer) * gelu_slope(inner)).astype(jnp.bfloat16)
        grad_b_inner = column_sum(grad_inner)
        grad_w_inner = product_tn(hidden_low, grad_inner)
        grad_hidden = grad_resid_two + product_nt(grad_inner, all_inner)
        grad_resid_one, grad_gain_one, grad_shift_one = normalize_back(
            grad_hidden, normed_one, inv_one, gain_a
        )
        grad_attn = grad_resid_one.astype(jnp.bfloat16)
        grad_b_out = column_sum(grad_attn)
        grad_w_out = product_tn(context, grad_attn)
        grad_context = (
            product_nt(grad_attn, all_out).astype(jnp.bfloat16).reshape(group, half, width)
        )
        probs_full = jnp.exp(score_table(queries, keys_all, visible) - log_total)
        grad_probs = jnp.einsum(
            "bqhd,bkhd->bhqk",
            split_heads(grad_context),
            split_heads(values_all),
            preferred_element_type=jnp.float32,
        )
        row_term = jnp.sum(probs_full * grad_probs, axis=-1, keepdims=True)
        grad_scores = (probs_full * (grad_probs - row_term)).astype(jnp.bfloat16)
        query_part = (
            jnp.einsum(
                "bhqk,bkhd->bqhd",
                grad_scores,
                split_heads(keys_all),
                preferred_element_type=jnp.float32,
            )
            * scale
        )
        query_part = query_part.reshape(group, att_len, att_width).astype(jnp.bfloat16)
        key_part = (
            jnp.einsum(
                "bhqk,bqhd->bkhd",
                grad_scores,
                split_heads(queries),
                preferred_element_type=jnp.float32,
            )
            * scale
        )
        value_part = jnp.einsum(
            "bhqk,bqhd->bkhd",
            probs_full.astype(jnp.bfloat16),
            split_heads(grad_context),
            preferred_element_type=jnp.float32,
        )
        key_part = key_part.reshape(group, full_len, att_width)
        value_part = value_part.reshape(group, full_len, att_width)
        grad_queries = query_part
        grad_keys, grad_values = (
            lax.psum_scatter(
                key_part.astype(jnp.bfloat16), "seq", scatter_dimension=1, tiled=True
            ).astype(jnp.float32),
            lax.psum_scatter(
                value_part.astype(jnp.bfloat16), "seq", scatter_dimension=1, tiled=True
            ).astype(jnp.float32),
        )
        grad_keys = grad_keys.astype(jnp.bfloat16)
        grad_values = grad_values.astype(jnp.bfloat16)
        grad_queries = grad_queries.reshape(rows, width)
        grad_keys = grad_keys.reshape(rows, width)
        grad_values = grad_values.reshape(rows, width)
        grad_b_query = column_sum(grad_queries)
        grad_w_query = product_tn(tok_rows, grad_queries)
        grad_w_key = product_tn(tok_rows, grad_keys)
        grad_b_value = column_sum(grad_values)
        grad_w_value = product_tn(tok_rows, grad_values)
        grad_tok = (
            grad_resid_one
            + product_nt(grad_queries, all_query)
            + product_nt(grad_keys, all_key)
            + product_nt(grad_values, all_value)
        )
        outputs.append(output.reshape(group, half, width))
        input_grads.append(grad_tok.reshape(group, half, width))
        local_grads = (
            grad_w_query,
            grad_b_query,
            grad_w_key,
            grad_w_value,
            grad_b_value,
            grad_w_out,
            grad_b_out,
            grad_gain_one,
            grad_shift_one,
            grad_w_inner,
            grad_b_inner,
            grad_w_outer,
            grad_b_outer,
            grad_gain_two,
            grad_shift_two,
        )
        owned = (
            lax.psum_scatter(local_grads[0], ("dp", "seq"), scatter_dimension=0, tiled=True),
            lax.psum_scatter(local_grads[1], ("dp", "seq"), scatter_dimension=0, tiled=True),
            lax.psum_scatter(local_grads[2], ("dp", "seq"), scatter_dimension=0, tiled=True),
            lax.psum_scatter(local_grads[3], ("dp", "seq"), scatter_dimension=0, tiled=True),
            lax.psum_scatter(local_grads[4], ("dp", "seq"), scatter_dimension=0, tiled=True),
            lax.psum_scatter(local_grads[5], ("dp", "seq"), scatter_dimension=0, tiled=True),
            lax.psum_scatter(local_grads[6], ("dp", "seq"), scatter_dimension=0, tiled=True),
            lax.psum_scatter(local_grads[7], ("dp", "seq"), scatter_dimension=0, tiled=True),
            lax.psum_scatter(local_grads[8], ("dp", "seq"), scatter_dimension=0, tiled=True),
            lax.psum_scatter(local_grads[9], ("dp", "seq"), scatter_dimension=0, tiled=True),
            lax.psum_scatter(local_grads[10], ("dp", "seq"), scatter_dimension=0, tiled=True),
            lax.psum_scatter(local_grads[11], ("dp", "seq"), scatter_dimension=0, tiled=True),
            lax.psum_scatter(local_grads[12], ("dp", "seq"), scatter_dimension=0, tiled=True),
            lax.psum_scatter(local_grads[13], ("dp", "seq"), scatter_dimension=0, tiled=True),
            lax.psum_scatter(local_grads[14], ("dp", "seq"), scatter_dimension=0, tiled=True),
        )
        totals = tuple((running + fresh for running, fresh in zip(totals, owned)))
    (
        g_query,
        gb_query,
        g_key,
        g_value,
        gb_value,
        g_out,
        gb_out,
        gg_one,
        gs_one,
        g_inner,
        gb_inner,
        g_outer,
        gb_outer,
        gg_two,
        gs_two,
    ) = totals
    return (
        jnp.concatenate(outputs, axis=0),
        jnp.concatenate(input_grads, axis=0),
        g_query,
        gb_query,
        g_key,
        g_value,
        gb_value,
        g_out,
        gb_out,
        gg_one,
        gs_one,
        g_inner,
        gb_inner,
        g_outer,
        gb_outer,
        gg_two,
        gs_two,
    )


def solution(mesh):
    return jax.shard_map(
        body,
        mesh=mesh,
        in_specs=(
            P("dp", "seq", None),
            P("dp"),
            P("dp", "seq", None),
            P(("dp", "seq"), None),
            P(("dp", "seq")),
            P(("dp", "seq"), None),
            P(("dp", "seq"), None),
            P(("dp", "seq")),
            P(("dp", "seq"), None),
            P(("dp", "seq")),
            P(("dp", "seq")),
            P(("dp", "seq")),
            P(("dp", "seq"), None),
            P(("dp", "seq")),
            P(("dp", "seq"), None),
            P(("dp", "seq")),
            P(("dp", "seq")),
            P(("dp", "seq")),
        ),
        out_specs=(
            P("dp", "seq", None),
            P("dp", "seq", None),
            P(("dp", "seq"), None),
            P(("dp", "seq")),
            P(("dp", "seq"), None),
            P(("dp", "seq"), None),
            P(("dp", "seq")),
            P(("dp", "seq"), None),
            P(("dp", "seq")),
            P(("dp", "seq")),
            P(("dp", "seq")),
            P(("dp", "seq"), None),
            P(("dp", "seq")),
            P(("dp", "seq"), None),
            P(("dp", "seq")),
            P(("dp", "seq")),
            P(("dp", "seq")),
        ),
        check_vma=False,
    )
```

profile of v0, /device:TPU:0, one launch (start us, length us, event | category | flops | bytes accessed | tf_op | source)
XLA Modules:
  0.0 1147.5 jit_solution(12268652226015138229)
XLA Ops:
  18.8 42.4 %all-reduce.19 = (bf16[768]{0:T(1024)(128)(2,1)S(1)}, bf16[768]{0:T(1024)(128)(2,1)S(1)}, bf16[768]{0:T(1024)(128)(2,1)S(1)}, bf16[768]{0:T(1024)(128)(2,1)S(1)}...) all-reduce(bf16[768]{0:T(1024)(128)(2,1)S(1)} %dynamic-update-slice, ...), channel_id=1, replica_groups=mesh['dp'=16,'seq'=2] {'dp','seq'}, use_global_device_ids=true, to_apply=%add | all-reduce | flops 9216 | bytes 36864
  74.1 49.9 %all-gather.11.cloned.1.call-done = bf16[768,768]{1,0:T(8,128)(2,1)} async-done(((bf16[24,768]{1,0:T(8,128)(2,1)}), bf16[768,768]{1,0:T(8,128)(2,1)}) %all-gather.11.cloned.1.call-update) | async-done | bytes 1179664 | tf_op jit(solution)/shard_map/all_gather | solution.py:137
  133.4 46.5 %all-gather.15.cloned.1.call-done = bf16[768,768]{1,0:T(8,128)(2,1)} async-done(((bf16[24,768]{1,0:T(8,128)(2,1)}), bf16[768,768]{1,0:T(8,128)(2,1)}) %all-gather.15.cloned.1.call-update) | async-done | bytes 1179664 | tf_op jit(solution)/shard_map/all_gather | solution.py:136
  184.9 2.6 all-gather.1
  195.1 40.5 %all-gather.17.cloned.1.call-done = bf16[768,768]{1,0:T(8,128)(2,1)} async-done(((bf16[24,768]{1,0:T(8,128)(2,1)}), bf16[768,768]{1,0:T(8,128)(2,1)}) %all-gather.17.cloned.1.call-update) | async-done | bytes 1179664 | tf_op jit(solution)/shard_map/all_gather | solution.py:139
  246.2 54.9 %all-gather.19.cloned.1.call-done = bf16[768,3072]{1,0:T(8,128)(2,1)} async-done(((bf16[24,3072]{1,0:T(8,128)(2,1)}), bf16[768,3072]{1,0:T(8,128)(2,1)}) %all-gather.19.cloned.1.call-update) | async-done | bytes 4718608 | tf_op jit(solution)/shard_map/all_gather | solution.py:143
  301.1 6.4 multiply_convert_fusion.3
  307.5 58.8 %all-gather.21.cloned.1.call-done = bf16[3072,768]{1,0:T(8,128)(2,1)} async-done(((bf16[96,768]{1,0:T(8,128)(2,1)}), bf16[3072,768]{1,0:T(8,128)(2,1)}) %all-gather.21.cloned.1.call-update) | async-done | bytes 4718608 | tf_op jit(solution)/shard_map/all_gather | solution.py:145
  366.4 4.4 fusion.122
  378.6 3.0 convert_reduce_fusion.1
  383.9 3.0 convert_reduce_fusion
  386.9 2.5 convert_reduce_fusion.5
  391.0 4.8 fusion.22
  398.5 5.3 fusion.25
  403.9 3.9 multiply_reduce_fusion.1
  407.9 3.7 multiply_convert_fusion.1
  413.2 4.4 multiply_reduce_fusion
  417.6 3.7 multiply_convert_fusion
  439.1 2.9 add_bitcast_fusion
  442.0 3.1 copy.80
  446.7 2.9 add_bitcast_fusion.1
  449.6 3.2 copy.78
  454.7 5.3 convolution_add_fusion.1
  463.6 4.7 convolution_add_fusion
  472.7 2.5 pad_maximum_fusion
  478.4 41.2 %all-reduce.18 = (f32[768]{0:T(1024)S(1)}, f32[768]{0:T(1024)S(1)}, f32[768]{0:T(1024)S(1)}, f32[768]{0:T(1024)S(1)}, f32[768]{0:T(1024)S(1)}, /*index=5*/f32[30...) all-reduce(f32[768]{0:T(1024)S(1)} %reshape.521, ...), channel_id=26, replica_groups=mesh['dp'=16,'seq'=2] {'dp','seq'}, use_global_device_ids=true, to_apply=%region_29.30.clone | all-reduce | flops 9216 | bytes 73728
  529.7 14.8 %reduce-scatter.25.cloned.1.call-done = f32[24,768]{1,0:T(8,128)} async-done(((f32[768,768]{1,0:T(8,128)}), f32[24,768]{1,0:T(8,128)}) %reduce-scatter.25.cloned.1.call-update) | async-done | bytes 73744 | tf_op jit(solution)/shard_map/reduce_scatter | solution.py:352
  544.5 104.6 %reduce-scatter.31.cloned.1.call-done = f32[24,768]{1,0:T(8,128)} async-done(((f32[768,768]{1,0:T(8,128)}), f32[24,768]{1,0:T(8,128)}) %reduce-scatter.31.cloned.1.call-update) | async-done | bytes 73744
  649.1 104.0 %reduce-scatter.35.cloned.1.call-done = f32[24,768]{1,0:T(8,128)} async-done(((f32[768,768]{1,0:T(8,128)}), f32[24,768]{1,0:T(8,128)}) %reduce-scatter.35.cloned.1.call-update) | async-done | bytes 73744
  753.1 104.6 %reduce-scatter.33.cloned.1.call-done = f32[24,768]{1,0:T(8,128)} async-done(((f32[768,768]{1,0:T(8,128)}), f32[24,768]{1,0:T(8,128)}) %reduce-scatter.33.cloned.1.call-update) | async-done | bytes 73744
  857.7 140.8 %reduce-scatter.27.cloned.1.call-done = f32[24,3072]{1,0:T(8,128)} async-done(((f32[768,3072]{1,0:T(8,128)}), f32[24,3072]{1,0:T(8,128)}) %reduce-scatter.27.cloned.1.call-update) | async-done | bytes 294928 | tf_op jit(solution)/shard_map/reduce_scatter | solution.py:356
  998.6 142.2 %reduce-scatter.29.cloned.1.call-done = f32[96,768]{1,0:T(8,128)} async-done(((f32[3072,768]{1,0:T(8,128)}), f32[96,768]{1,0:T(8,128)}) %reduce-scatter.29.cloned.1.call-update) | async-done | bytes 294928 | tf_op jit(solution)/shard_map/reduce_scatter | solution.py:358
  (386 shorter events, 114.1 us)
Async XLA Ops:
  7.2 64.2 %copy-start.14 = (bf16[2,256,768]{2,1,0:T(8,128)(2,1)S(1)}, bf16[2,256,768]{2,1,0:T(8,128)(2,1)}, u32[]{:S(2)}) copy-start(bf16[2,256,768]{2,1,0:T(8,128)(2,1)} %param.18) | copy-start | bytes 2359300
  7.2 61.3 %all-gather.13.cloned.1.call-start = ((), (), s32[]{:S(2)}) async-start(), calls=%async_computation.11 | async-start | bytes 1216512 | tf_op jit(solution)/shard_map/all_gather | solution.py:134
  7.9 116.1 %all-gather.11.cloned.1.call-start = ((), (), s32[]{:S(2)}) async-start(), calls=%async_computation.10 | async-start | bytes 1216512 | tf_op jit(solution)/shard_map/all_gather | solution.py:137
  8.7 171.2 %all-gather.15.cloned.1.call-start = ((), (), s32[]{:S(2)}) async-start(), calls=%async_computation.12 | async-start | bytes 1216512 | tf_op jit(solution)/shard_map/all_gather | solution.py:136
  9.4 226.3 %all-gather.17.cloned.1.call-start = ((), (), s32[]{:S(2)}) async-start(), calls=%async_computation.13 | async-start | bytes 1216512 | tf_op jit(solution)/shard_map/all_gather | solution.py:139
  10.0 291.1 %all-gather.19.cloned.1.call-start = ((), (), s32[]{:S(2)}) async-start(), calls=%async_computation.14 | async-start | bytes 4866048 | tf_op jit(solution)/shard_map/all_gather | solution.py:143
  10.6 355.7 %all-gather.21.cloned.1.call-start = ((), (), s32[]{:S(2)}) async-start(), calls=%async_computation.15 | async-start | bytes 4866048 | tf_op jit(solution)/shard_map/all_gather | solution.py:145
  11.2 426.4 %reduce-scatter.19.cloned.1.call-start = ((), (), s32[]{:S(2)}) async-start(), calls=%async_computation.17 | async-start | bytes 1179648 | tf_op jit(solution)/shard_map/reduce_scatter | solution.py:307
  184.4 54.1 %copy-start.11 = (bf16[512,768]{0,1:T(8,128)(2,1)}, bf16[512,768]{0,1:T(8,128)(2,1)S(1)}, u32[]{:S(2)}) copy-start(bf16[512,768]{0,1:T(8,128)(2,1)S(1)} %copy.70) | copy-start | bytes 2359300
  195.1 44.5 %copy-start.55 = (bf16[12,64,256]{2,1,0:T(8,128)(2,1)}, bf16[12,64,256]{2,1,0:T(8,128)(2,1)S(1)}, u32[]{:S(2)}) copy-start(bf16[12,64,256]{2,1,0:T(8,128)(2,1)S(1)} %fusion.41) | copy-start | bytes 1179652
  195.1 43.4 %copy-start.30 = (bf16[256,768]{0,1:T(8,128)(2,1)S(1)}, bf16[256,768]{0,1:T(8,128)(2,1)}, u32[]{:S(2)}) copy-start(bf16[256,768]{0,1:T(8,128)(2,1)} %copy.69) | copy-start | bytes 1179652
  195.1 43.4 %copy-start.106 = (pred[512]{0:T(512)(128)(4,1)S(1)}, pred[512]{0:T(512)(128)(4,1)}, u32[]{:S(2)}) copy-start(pred[512]{0:T(512)(128)(4,1)} %iota_compare_fusion) | copy-start | bytes 1540
  244.6 56.5 %copy-start.43 = (f32[256,768]{1,0:T(8,128)S(1)}, f32[256,768]{1,0:T(8,128)}, u32[]{:S(2)}) copy-start(f32[256,768]{1,0:T(8,128)} %copy-done.42) | copy-start | bytes 2359300
  245.3 150.8 %copy-start.7 = (f32[256,768]{1,0:T(8,128)}, f32[256,768]{1,0:T(8,128)S(1)}, u32[]{:S(2)}) copy-start(f32[256,768]{1,0:T(8,128)S(1)} %get-tuple-element.127) | copy-start | bytes 2359300
  245.3 150.8 %copy-start.72 = (f32[256]{0:T(256)}, f32[256]{0:T(256)S(1)}, u32[]{:S(2)}) copy-start(f32[256]{0:T(256)S(1)} %broadcast_multiply_fusion.9) | copy-start | bytes 3076
  245.5 120.8 %copy-start.95 = (f32[256]{0:T(256)}, f32[256]{0:T(256)S(1)}, u32[]{:S(2)}) copy-start(f32[256]{0:T(256)S(1)} %add_rsqrt_fusion.3) | copy-start | bytes 3076
  245.6 126.8 %copy-start.86 = (f32[256]{0:T(256)}, f32[256]{0:T(256)S(1)}, u32[]{:S(2)}) copy-start(f32[256]{0:T(256)S(1)} %add_rsqrt_fusion.1) | copy-start | bytes 3076
  246.2 120.1 %copy-start.83 = (f32[256]{0:T(256)S(1)}, f32[256]{0:T(256)}, u32[]{:S(2)}) copy-start(f32[256]{0:T(256)} %copy-done.82) | copy-start | bytes 3076
  246.2 120.1 %copy-start.103 = (f32[768]{0:T(1024)S(1)}, f32[768]{0:T(1024)}, u32[]{:S(2)}) copy-start(f32[768]{0:T(1024)} %convert_element_type.359) | copy-start | bytes 9220
  372.4 11.5 %copy-start.40 = (f32[256,3072]{1,0:T(8,128)}, f32[256,3072]{1,0:T(8,128)S(1)}, u32[]{:S(2)}) copy-start(f32[256,3072]{1,0:T(8,128)S(1)} %convolution_add_fusion.2) | copy-start | bytes 9437188
  395.9 43.2 %reduce-scatter.23.cloned.1.call-start = ((), (), s32[]{:S(2)}) async-start(), calls=%async_computation.19 | async-start | bytes 1179648 | tf_op jit(solution)/shard_map/reduce_scatter | solution.py:307
  403.8 41.4 %reduce-scatter.17.cloned.1.call-start = ((), (), s32[]{:S(2)}) async-start(), calls=%async_computation.16 | async-start | bytes 1179648 | tf_op jit(solution)/shard_map/reduce_scatter | solution.py:304
  413.1 33.6 %reduce-scatter.21.cloned.1.call-start = ((), (), s32[]{:S(2)}) async-start(), calls=%async_computation.18 | async-start | bytes 1179648 | tf_op jit(solution)/shard_map/reduce_scatter | solution.py:304
  424.5 120.1 %reduce-scatter.25.cloned.1.call-start = ((), (), s32[]{:S(2)}) async-start(), calls=%async_computation.20 | async-start | bytes 2433024 | tf_op jit(solution)/shard_map/reduce_scatter | solution.py:352
  428.2 220.9 %reduce-scatter.31.cloned.1.call-start = ((), (), s32[]{:S(2)}) async-start(), calls=%async_computation.23 | async-start | bytes 2433024
  437.5 315.6 %reduce-scatter.35.cloned.1.call-start = ((), (), s32[]{:S(2)}) async-start(), calls=%async_computation.25 | async-start | bytes 2433024
  445.2 412.6 %reduce-scatter.33.cloned.1.call-start = ((), (), s32[]{:S(2)}) async-start(), calls=%async_computation.24 | async-start | bytes 2433024
  452.9 545.6 %reduce-scatter.27.cloned.1.call-start = ((), (), s32[]{:S(2)}) async-start(), calls=%async_computation.21 | async-start | bytes 9732096 | tf_op jit(solution)/shard_map/reduce_scatter | solution.py:356
  460.0 680.7 %reduce-scatter.29.cloned.1.call-start = ((), (), s32[]{:S(2)}) async-start(), calls=%async_computation.22 | async-start | bytes 9732096 | tf_op jit(solution)/shard_map/reduce_scatter | solution.py:358
  475.2 49.7 %copy-start.19 = (bf16[768,768]{1,0:T(8,128)(2,1)S(1)}, bf16[768,768]{1,0:T(8,128)(2,1)}, u32[]{:S(2)}) copy-start(bf16[768,768]{1,0:T(8,128)(2,1)} %all-gather.15.cloned.1.call-done) | copy-start | bytes 3538948
  476.6 50.2 %copy-start.17 = (bf16[768,768]{1,0:T(8,128)(2,1)S(1)}, bf16[768,768]{1,0:T(8,128)(2,1)}, u32[]{:S(2)}) copy-start(bf16[768,768]{1,0:T(8,128)(2,1)} %all-gather.11.cloned.1.call-done) | copy-start | bytes 3538948
  478.0 48.8 %copy-start.25 = (bf16[1,256,768]{1,2,0:T(8,128)(2,1)S(1)}, bf16[1,256,768]{1,2,0:T(8,128)(2,1)}, u32[]{:S(2)}) copy-start(bf16[1,256,768]{1,2,0:T(8,128)(2,1)} %reduce-scatter.19.cloned.1.call-done) | copy-start | bytes 1179652
  (95 other events, 285.0 us)
Sparse Core Ops, SparseCore 0:
  10.9 56.9 all-gather.12
  70.8 53.1 all-gather.10
  126.9 52.9 all-gather.14
  182.6 52.9 all-gather.16
  238.4 62.6 all-gather.18
  303.8 62.4 all-gather.20
  396.0 7.0 reduce-scatter.18
  405.4 9.3 reduce-scatter.22
  417.1 9.4 reduce-scatter.16
  428.7 9.3 reduce-scatter.20
  444.1 100.4 reduce-scatter.24
  551.1 97.9 reduce-scatter.30
  655.0 98.0 reduce-scatter.34
  759.7 98.0 reduce-scatter.32
  864.1 134.4 reduce-scatter.26
  1005.9 134.7 reduce-scatter.28
where the time goes:
time: 1150 us
  waiting for transfers between devices  866 us (75%)
  matrix products  104 us (9%)
  blocking collectives  93.4 us (8%)
  local copies, waits for them, and re-layouts  37.8 us (3%)
  other arithmetic  30.5 us (3%)
  between operations  15.7 us (1%)
    unnamed x19, waiting for transfers between devices  317 us
    reduce_scatter x1, waiting for transfers between devices, body(): lax.psum_scatter(local_grads[11], ('dp', 'seq'), scatter_dimension=0, til...  142 us
    reduce_scatter x1, waiting for transfers between devices, body(): lax.psum_scatter(local_grads[9], ('dp', 'seq'), scatter_dimension=0, tile...  141 us
    unnamed x2, blocking collectives  83.7 us
    all_gather x1, waiting for transfers between devices, body(): lax.all_gather(shards[11], ('dp', 'seq'), axis=0, tiled=True)  58.8 us
    all_gather x1, waiting for transfers between devices, body(): lax.all_gather(shards[9], ('dp', 'seq'), axis=0, tiled=True)  54.9 us
    all_gather x1, waiting for transfers between devices, body(): lax.all_gather(shards[3], ('dp', 'seq'), axis=0, tiled=True)  49.9 us
    all_gather x1, waiting for transfers between devices, body(): lax.all_gather(shards[2], ('dp', 'seq'), axis=0, tiled=True)  46.5 us
  transfers between devices with their start and end apart: 16, of which 11 were waited for; matrix products, arithmetic and copies ran while one was open for 12% of the time, Pallas kernels for 0%

commit v1 on v0

v1 whole, which is shorter than its diff:
```python
import jax
import jax.numpy as jnp
from jax import lax
from jax.experimental import pallas as pl
from jax.experimental.pallas import tpu as pltpu
from jax.sharding import PartitionSpec as P

HEAD_DIM = 64
PAIR = 2 * HEAD_DIM
NEG_BIG = -1000000000.0
EPSILON = 1e-05
ROOT_HALF = 0.7071067811865476
INV_ROOT_TAU = 0.3989422804014327
BF = jnp.bfloat16
F32 = jnp.float32


def product(left, right):
    return jnp.dot(left, right, preferred_element_type=F32)


def product_tn(left, right):
    return lax.dot_general(left, right, (((0,), (0,)), ((), ())), preferred_element_type=F32)


def product_nt(left, right):
    return lax.dot_general(left, right, (((1,), (1,)), ((), ())), preferred_element_type=F32)


def column_sum(values):
    return jnp.sum(values, axis=0, dtype=F32)


def normalize_keep(values, gain, shift):
    center = values - jnp.mean(values, axis=-1, keepdims=True)
    inv_spread = lax.rsqrt(jnp.mean(center * center, axis=-1, keepdims=True) + EPSILON)
    normed = center * inv_spread
    return (normed * gain + shift, normed, inv_spread)


def normalize_back(grad_out, normed, inv_spread, gain):
    grad_normed = grad_out * gain
    centered = grad_normed - jnp.mean(grad_normed, axis=-1, keepdims=True)
    grad_in = inv_spread * (
        centered - normed * jnp.mean(grad_normed * normed, axis=-1, keepdims=True)
    )
    return (grad_in, jnp.sum(grad_out * normed, axis=0), jnp.sum(grad_out, axis=0))


def attend_kernel(len_ref, q_ref, k_ref, v_ref, out_ref, lse_ref):
    count = len_ref[pl.program_id(0)]
    queries = q_ref[...] * BF(HEAD_DIM ** (-0.5))
    keys = k_ref[...]
    values_t = v_ref[...].T
    length = keys.shape[0]
    lane = lax.broadcasted_iota(jnp.int32, keys.shape, 1)
    seen = lax.broadcasted_iota(jnp.int32, (length, length), 0) < count
    parts = []
    for head in range(2):
        own = (lane >= head * HEAD_DIM) & (lane < (head + 1) * HEAD_DIM)
        scores = product_nt(jnp.where(own, keys, BF(0)), queries)
        scores = jnp.where(seen, scores, NEG_BIG)
        top = jnp.max(scores, axis=0, keepdims=True)
        weights = jnp.exp(scores - top)
        total = jnp.sum(weights, axis=0, keepdims=True)
        probs = (weights * (1.0 / total)).astype(BF)
        parts.append(product(values_t[head * HEAD_DIM : (head + 1) * HEAD_DIM], probs))
        lse_ref[0, 0, head : head + 1, :] = top + jnp.log(total)
    out_ref[...] = jnp.concatenate(parts, axis=0).T.astype(BF)


def attend_back_kernel(len_ref, q_ref, k_ref, v_ref, g_ref, lse_ref, dq_ref, dk_ref, dv_ref):
    count = len_ref[pl.program_id(0)]
    scale = BF(HEAD_DIM ** (-0.5))
    queries = q_ref[...] * scale
    keys = k_ref[...]
    values = v_ref[...]
    grad = g_ref[...]
    keys_t = (keys * scale).T
    length = keys.shape[0]
    lane = lax.broadcasted_iota(jnp.int32, keys.shape, 1)
    seen = lax.broadcasted_iota(jnp.int32, (length, length), 0) < count
    dq, dk, dv = [], [], []
    for head in range(2):
        own = (lane >= head * HEAD_DIM) & (lane < (head + 1) * HEAD_DIM)
        scores = product_nt(jnp.where(own, keys, BF(0)), queries)
        scores = jnp.where(seen, scores, NEG_BIG)
        probs = jnp.exp(scores - lse_ref[0, 0, head : head + 1, :])
        grad_probs = product_nt(jnp.where(own, values, BF(0)), grad)
        row_term = jnp.sum(probs * grad_probs, axis=0, keepdims=True)
        grad_scores = (probs * (grad_probs - row_term)).astype(BF)
        dv.append(product(probs.astype(BF), grad))
        dk.append(product(grad_scores, queries))
        dq.append(product(keys_t[head * HEAD_DIM : (head + 1) * HEAD_DIM], grad_scores))
    first = lane < HEAD_DIM
    dv_ref[...] = jnp.where(first, dv[0], dv[1]).astype(BF)
    dk_ref[...] = jnp.where(first, dk[0], dk[1]).astype(BF)
    dq_ref[...] = jnp.concatenate(dq, axis=0).T.astype(BF)


def attention_specs(length, pairs):
    def at(offset):
        return pl.BlockSpec((length, PAIR), lambda s, p, n: (s, offset + p))

    lse = pl.BlockSpec((1, 1, 2, length), lambda s, p, n: (s, p, 0, 0))
    return at, lse


def attend(lengths, query_key, values, length):
    rows, width = values.shape
    pairs = width // PAIR
    seqs = rows // length
    at, lse = attention_specs(length, pairs)
    return pl.pallas_call(
        attend_kernel,
        out_shape=(
            jax.ShapeDtypeStruct((rows, width), BF),
            jax.ShapeDtypeStruct((seqs, pairs, 2, length), F32),
        ),
        grid_spec=pltpu.PrefetchScalarGridSpec(
            num_scalar_prefetch=1,
            grid=(seqs, pairs),
            in_specs=[at(0), at(pairs), at(0)],
            out_specs=(at(0), lse),
        ),
        compiler_params=pltpu.CompilerParams(vmem_limit_bytes=32 << 20),
        cost_estimate=pl.CostEstimate(
            flops=4 * rows * length * width,
            transcendentals=rows * length * width // HEAD_DIM,
            bytes_accessed=8 * rows * width,
        ),
        name="attend",
    )(lengths, query_key, query_key, values)


def attend_back(lengths, query_key, values, grad, lse_all, length):
    rows, width = values.shape
    pairs = width // PAIR
    seqs = rows // length
    at, lse = attention_specs(length, pairs)
    shape = jax.ShapeDtypeStruct((rows, width), BF)
    return pl.pallas_call(
        attend_back_kernel,
        out_shape=(shape, shape, shape),
        grid_spec=pltpu.PrefetchScalarGridSpec(
            num_scalar_prefetch=1,
            grid=(seqs, pairs),
            in_specs=[at(0), at(pairs), at(0), at(0), lse],
            out_specs=(at(0), at(0), at(0)),
        ),
        compiler_params=pltpu.CompilerParams(vmem_limit_bytes=32 << 20),
        cost_estimate=pl.CostEstimate(
            flops=10 * rows * length * width,
            transcendentals=rows * length * width // HEAD_DIM,
            bytes_accessed=14 * rows * width,
        ),
        name="attend_back",
    )(lengths, query_key, query_key, values, grad, lse_all)


class Wires:
    def __init__(self):
        self.chips = lax.axis_size("dp")
        self.bits = self.chips.bit_length() - 1
        self.chip = lax.axis_index("dp")
        self.core = lax.axis_index("seq")

    def side(self, bit):
        return (self.chip >> bit) & 1

    def swap(self, values, bit):
        return lax.ppermute(values, "dp", [(i, i ^ (1 << bit)) for i in range(self.chips)])

    def swap_core(self, values):
        return lax.ppermute(values, "seq", [(0, 1), (1, 0)])

    def beside(self, mine, theirs, side, axis):
        shape = [1] * (mine.ndim + 1)
        shape[axis] = 2
        here = jnp.arange(2).reshape(shape) == side
        return jnp.where(here, jnp.expand_dims(mine, axis), jnp.expand_dims(theirs, axis))

    def orders(self):
        far = list(range(self.bits - 1, -1, -1))
        return far, far[:-2] + [far[-1], far[-2]]

    def gather(self, values, order, flip=None):
        held = []
        for bit in order:
            other = self.swap(values, bit)
            axis = sum(1 for one in held if one > bit)
            side = self.side(bit)
            if flip is not None and bit == self.bits - 1:
                side = side ^ flip
            values = self.beside(values, other, side, axis)
            held.append(bit)
        return values.reshape(-1, values.shape[-1])

    def scatter(self, values, order, flip=None):
        left = list(range(self.bits - 1, -1, -1))
        values = values.reshape([2] * self.bits + [-1, values.shape[-1]])
        for step, bit in enumerate(reversed(order)):
            axis = left.index(bit)
            left.remove(bit)
            side = self.side(bit)
            if flip is not None and bit == self.bits - 1:
                side = side ^ flip
            away = lax.dynamic_index_in_dim(values, 1 - side, axis, keepdims=False)
            keep = lax.dynamic_index_in_dim(values, side, axis, keepdims=False)
            other = self.swap(away.astype(BF), bit)
            values = keep.astype(F32) + other.astype(F32)
            if left:
                values = values.astype(BF)
        return values

    def halves(self, shard):
        rows, width = shard.shape
        split = shard.reshape(rows, 2, width // 2)
        mine = lax.dynamic_index_in_dim(split, self.core, 1, keepdims=False)
        away = lax.dynamic_index_in_dim(split, 1 - self.core, 1, keepdims=False)
        return mine, away

    def paired(self, mine, theirs):
        return self.beside(mine, theirs, self.core, 0).reshape(-1, mine.shape[-1])

    def unpaired(self, block):
        split = block.reshape(2, -1, block.shape[-1])
        mine = lax.dynamic_index_in_dim(split, self.core, 0, keepdims=False)
        away = lax.dynamic_index_in_dim(split, 1 - self.core, 0, keepdims=False)
        theirs = self.swap_core(away)
        return self.beside(mine, theirs, self.core, 1).reshape(mine.shape[0], -1)

    def total(self, values):
        values = values + self.swap_core(values)
        for bit in range(self.bits):
            values = values + self.swap(values, bit)
        return values


def body(
    tokens,
    lengths,
    cotangent,
    w_query,
    b_query,
    w_key,
    w_value,
    b_value,
    w_out,
    b_out,
    gain_one,
    shift_one,
    w_inner,
    b_inner,
    w_outer,
    b_outer,
    gain_two,
    shift_two,
):
    wires = Wires()
    core = wires.core
    devices = 2 * wires.chips
    device = 2 * wires.chip + core
    seqs, half, width = tokens.shape
    length = 2 * half
    rows = seqs * half
    order_one, order_two = wires.orders()

    vectors = (b_query, b_value, b_out, gain_one, shift_one, b_outer, gain_two, shift_two)
    slot = b_query.shape[0]
    inner_slot = b_inner.shape[0]
    packed = jnp.concatenate(vectors + (b_inner,))
    packed = jnp.pad(packed, (0, -packed.shape[0] % 128))
    own_row = jnp.arange(devices)[:, None] == device
    packed = wires.total(jnp.where(own_row, packed[None, :], BF(0)))
    spread = [
        packed[:, i * slot : (i + 1) * slot].reshape(1, width).astype(F32)
        for i in range(len(vectors))
    ]
    bias_query, bias_value, bias_out, gain_a, shift_a, bias_outer, gain_b, shift_b = spread
    bias_inner = packed[:, len(vectors) * slot : len(vectors) * slot + inner_slot]
    bias_inner = bias_inner.reshape(1, -1).astype(F32)

    q_mine, q_away = wires.halves(w_query)
    k_mine, k_away = wires.halves(w_key)
    v_mine, v_away = wires.halves(w_value)
    first = jnp.concatenate([q_mine, k_mine, v_mine], axis=1)
    first_away = jnp.concatenate([q_away, k_away, v_away], axis=1)
    first = wires.paired(first, wires.swap_core(first_away))
    cols = width // 2
    w_qk = wires.gather(first[:, : 2 * cols], order_one)
    w_v = wires.gather(first[:, 2 * cols :], order_two)

    o_mine, o_away = wires.halves(w_out)
    w_out_mine = wires.gather(wires.paired(o_mine, wires.swap_core(o_away)), order_two)
    i_mine, i_away = wires.halves(w_inner)
    w_inner_mine = wires.gather(wires.paired(i_mine, wires.swap_core(i_away)), order_one)
    u_mine, u_away = wires.halves(w_outer)
    w_outer_mine = wires.gather(wires.paired(u_mine, wires.swap_core(u_away)), order_two, flip=core)
    w_out_theirs = wires.swap_core(w_out_mine)
    w_inner_theirs = wires.swap_core(w_inner_mine)
    hidden_units = w_inner_mine.shape[1] * 2
    outer_theirs = wires.swap_core(w_outer_mine)
    w_outer_theirs = jnp.concatenate(
        [outer_theirs[hidden_units // 2 :], outer_theirs[: hidden_units // 2]], axis=0
    )

    def natural(mine, theirs):
        return wires.beside(mine, theirs, core, 1).reshape(mine.shape[0], -1)

    def own_columns(values):
        split = values.reshape(values.shape[0], 2, -1)
        mine = lax.dynamic_index_in_dim(split, core, 1, keepdims=False)
        theirs = lax.dynamic_index_in_dim(split, 1 - core, 1, keepdims=False)
        return mine, theirs

    def all_positions(mine):
        theirs = wires.swap_core(mine)
        return wires.beside(mine, theirs, core, 1).reshape(seqs * length, -1)

    def split_positions(values):
        split = values.reshape(seqs, 2, half, -1)
        mine = lax.dynamic_index_in_dim(split, core, 1, keepdims=False)
        away = lax.dynamic_index_in_dim(split, 1 - core, 1, keepdims=False)
        return mine, away

    tok_rows = tokens.reshape(rows, width)
    tok_all = all_positions(tokens)
    bias_q, _ = own_columns(bias_query)
    bias_v, _ = own_columns(bias_value)
    bias_qk = jnp.concatenate([bias_q, jnp.zeros_like(bias_q)], axis=1)
    query_key = (product(tok_all, w_qk) + bias_qk).astype(BF)
    values = (product(tok_all, w_v) + bias_v).astype(BF)
    context_heads, lse = attend(lengths, query_key, values, length)
    ctx_mine, ctx_away = split_positions(context_heads)
    ctx_theirs = wires.swap_core(ctx_away)
    context = natural(ctx_mine.reshape(rows, -1), ctx_theirs.reshape(rows, -1))
    attn_out = natural(product(context, w_out_mine), product(context, w_out_theirs)) + bias_out
    hidden, normed_one, inv_one = normalize_keep(tok_rows.astype(F32) + attn_out, gain_a, shift_a)
    hidden_low = hidden.astype(BF)
    bias_in = own_columns(bias_inner)
    inner, active, slope = [], [], []
    for weight, bias in zip((w_inner_mine, w_inner_theirs), bias_in):
        pre = product(hidden_low, weight) + bias
        cumulative = 0.5 * (1.0 + lax.erf(pre * ROOT_HALF))
        active.append((pre * cumulative).astype(BF))
        slope.append((cumulative + pre * jnp.exp(-0.5 * pre * pre) * INV_ROOT_TAU).astype(BF))
    active = jnp.concatenate(active, axis=1)
    outer = natural(product(active, w_outer_mine), product(active, w_outer_theirs)) + bias_outer
    output, normed_two, inv_two = normalize_keep(hidden + outer, gain_b, shift_b)

    positions = core * half + jnp.arange(half, dtype=jnp.int32)
    live = (positions[None, :] < lengths[:, None]).astype(F32).reshape(rows, 1)
    grad_y = cotangent.reshape(rows, width).astype(F32) * live
    grad_resid_two, grad_gain_two, grad_shift_two = normalize_back(
        grad_y, normed_two, inv_two, gain_b
    )
    grad_outer = grad_resid_two.astype(BF)
    grad_b_outer = column_sum(grad_outer)
    go_mine, go_theirs = own_columns(grad_outer)
    g_outer = product_tn(active, go_mine).astype(BF)
    g_outer_away = product_tn(active, go_theirs).astype(BF)
    g_outer_away = jnp.concatenate(
        [g_outer_away[hidden_units // 2 :], g_outer_away[: hidden_units // 2]], axis=0
    )
    g_outer = g_outer.astype(F32) + wires.swap_core(g_outer_away).astype(F32)
    g_outer = wires.scatter(g_outer.astype(BF), order_two, flip=core)

    grad_active = product_nt(go_mine, w_outer_mine) + product_nt(go_theirs, w_outer_theirs)
    part = hidden_units // 2
    grad_inner = [
        (grad_active[:, i * part : (i + 1) * part] * slope[i].astype(F32)).astype(BF)
        for i in range(2)
    ]
    sums_inner = [column_sum(one) for one in grad_inner]
    grad_b_inner = natural(sums_inner[0][None], sums_inner[1][None]).reshape(-1)
    g_inner_away = wires.swap_core(product_tn(hidden_low, grad_inner[1]).astype(BF))
    g_inner = product_tn(hidden_low, grad_inner[0]).astype(BF)
    g_inner = g_inner.astype(F32) + g_inner_away.astype(F32)
    g_inner = wires.scatter(g_inner.astype(BF), order_one)

    grad_hidden = (
        grad_resid_two
        + product_nt(grad_inner[0], w_inner_mine)
        + product_nt(grad_inner[1], w_inner_theirs)
    )
    grad_resid_one, grad_gain_one, grad_shift_one = normalize_back(
        grad_hidden, normed_one, inv_one, gain_a
    )
    grad_attn = grad_resid_one.astype(BF)
    grad_b_out = column_sum(grad_attn)
    ga_mine, ga_theirs = own_columns(grad_attn)
    grad_context = product_nt(ga_mine, w_out_mine) + product_nt(ga_theirs, w_out_theirs)
    gc_mine, gc_theirs = own_columns(grad_context.astype(BF))
    gc_other = wires.swap_core(gc_theirs)
    grad_heads = wires.beside(
        gc_mine.reshape(seqs, half, -1), gc_other.reshape(seqs, half, -1), core, 1
    ).reshape(seqs * length, -1)
    g_out_away = wires.swap_core(product_tn(context, ga_theirs).astype(BF))
    g_out = product_tn(context, ga_mine).astype(BF)
    g_out = g_out.astype(F32) + g_out_away.astype(F32)
    g_out = wires.scatter(g_out.astype(BF), order_two)

    dq, dk, dv = attend_back(lengths, query_key, values, grad_heads, lse, length)
    g_qk = jnp.concatenate(
        [product_tn(tok_all, dq).astype(BF), product_tn(tok_all, dk).astype(BF)], axis=1
    )
    g_qk = wires.scatter(g_qk, order_one)
    g_v = wires.scatter(product_tn(tok_all, dv).astype(BF), order_two)

    zero = jnp.zeros((cols,), F32)
    sum_q = natural_half(column_sum(dq), zero, core)
    sum_v = natural_half(column_sum(dv), zero, core)
    sums = jnp.stack(
        [
            sum_q,
            sum_v,
            grad_b_out,
            grad_gain_one,
            grad_shift_one,
            grad_b_outer,
            grad_gain_two,
            grad_shift_two,
        ]
    )
    sums = jnp.concatenate([sums, grad_b_inner.reshape(-1, width)], axis=0)
    sums = wires.total(sums)
    small = lax.dynamic_index_in_dim(
        sums[: len(vectors)].reshape(len(vectors), devices, slot), device, 1, keepdims=False
    )
    small_inner = lax.dynamic_index_in_dim(
        sums[len(vectors) :].reshape(devices, inner_slot), device, 0, keepdims=False
    )

    partial = (
        product_nt(dq, w_qk[:, :cols]) + product_nt(dk, w_qk[:, cols:]) + product_nt(dv, w_v)
    )
    part_mine, part_away = split_positions(partial)
    part_theirs = wires.swap_core(part_away.astype(BF))
    grad_tok = (
        grad_resid_one
        + part_mine.reshape(rows, width)
        + part_theirs.reshape(rows, width).astype(F32)
    )

    w_cols = jnp.concatenate([g_qk, g_v, g_out, g_inner], axis=1)
    w_grads = wires.unpaired(w_cols)
    at = [0, cols, 2 * cols, 3 * cols, 4 * cols, 4 * cols + part]
    w_grads = w_grads.reshape(slot, 2, -1)
    pieces = [w_grads[:, :, at[i] : at[i + 1]].reshape(slot, -1) for i in range(5)]
    outer_grad = wires.unpaired(g_outer)

    return (
        output.reshape(seqs, half, width),
        grad_tok.reshape(seqs, half, width),
        pieces[0],
        small[0],
        pieces[1],
        pieces[2],
        small[1],
        pieces[3],
        small[2],
        small[3],
        small[4],
        pieces[4],
        small_inner,
        outer_grad,
        small[5],
        small[6],
        small[7],
    )


def natural_half(mine, zero, core):
    here = jnp.arange(2)[:, None] == core
    return jnp.where(here, mine[None], zero[None]).reshape(-1)


def solution(mesh):
    every = ("dp", "seq")
    matrix, vector = P(every, None), P(every)
    rows = P("dp", "seq", None)
    kinds = (matrix, vector, matrix, matrix, vector, matrix, vector, vector, vector, matrix, vector, matrix, vector, vector, vector)
    return jax.shard_map(
        body,
        mesh=mesh,
        in_specs=(rows, P("dp"), rows) + kinds,
        out_specs=(rows, rows) + kinds,
        check_vma=False,
    )
```

time: 1150 us -> 449 us (0.39)
  waiting for transfers between devices: 866 us -> 109 us
  blocking collectives: 93.4 us -> 0 us
  local copies, waits for them, and re-layouts: 37.8 us -> 118 us
  starting transfers between devices: 0.81 us -> 64.9 us
  matrix products: 104 us -> 64.9 us
  other arithmetic: 30.5 us -> 61 us
  Pallas kernels: 0 us -> 22.5 us
  between operations: 15.7 us -> 2.94 us
    unnamed x19 -> x0, waiting for transfers between devices: 317 us -> none
    reduce_scatter x7 -> x0, waiting for transfers between devices: 298 us -> none  [the longest x1 142 us: body(): lax.psum_scatter(local_grads[11], ('dp', 'seq'), scatter_dimension=0, til...]
    all_gather x6 -> x0, waiting for transfers between devices: 251 us -> none  [the longest x1 58.8 us: body(): lax.all_gather(shards[11], ('dp', 'seq'), axis=0, tiled=True)]
    ppermute x0 -> x66, waiting for transfers between devices: none -> 109 us  [the longest x48 109 us: swap(): lax.ppermute(values, 'dp', [(i, i ^ 1 << bit) for i in range(self.chips)])]
    unnamed x2 -> x0, blocking collectives: 83.7 us -> none
    ppermute x0 -> x66, starting transfers between devices: none -> 64.9 us  [the longest x48 61.3 us: swap(): lax.ppermute(values, 'dp', [(i, i ^ 1 << bit) for i in range(self.chips)])]
    broadcast_in_dim x0 -> x47, local copies, waits for them, and re-layouts: none -> 62.3 us  [beside(): jnp.where(here, jnp.expand_dims(mine, axis), jnp.expand_dims(theirs, axis))]
    dot_general x24 -> x8, matrix products: 58.3 us -> 15.9 us  [product(): return jnp.dot(left, right, preferred_element_type=F32)]
  transfers between devices with their start and end apart: 16 -> 66, of which waited for: 11 -> 27; matrix products, arithmetic and copies ran while one was open for 12% -> 36% of each run, Pallas kernels for 0% -> 5%
where the time goes in v1:
time: 449 us; the launch traced here: 443 us
  local copies, waits for them, and re-layouts  118 us (26%)
  waiting for transfers between devices  109 us (24%)
  starting transfers between devices  64.9 us (14%)
  matrix products  64.9 us (14%)
  other arithmetic  61 us (14%)
  Pallas kernels  22.5 us (5%)
    ppermute x48, waiting for transfers between devices, swap(): lax.ppermute(values, 'dp', [(i, i ^ 1 << bit) for i in range(self.chips)])  109 us
    broadcast_in_dim x47, local copies, waits for them, and re-layouts, beside(): jnp.where(here, jnp.expand_dims(mine, axis), jnp.expand_dims(theirs, axis))  62.3 us
    ppermute x48, starting transfers between devices, swap(): lax.ppermute(values, 'dp', [(i, i ^ 1 << bit) for i in range(self.chips)])  61.3 us
    select_n x31, other arithmetic, beside(): jnp.where(here, jnp.expand_dims(mine, axis), jnp.expand_dims(theirs, axis))  30.1 us
    dot_general x9, matrix products, product_nt(): lax.dot_general(left, right, (((1,), (1,)), ((), ())), preferred_element_...  27.8 us
    dot_general x9, matrix products, product_tn(): lax.dot_general(left, right, (((0,), (0,)), ((), ())), preferred_element_...  21.1 us
    dot_general x8, matrix products, product(): return jnp.dot(left, right, preferred_element_type=F32)  15.9 us
    unnamed x200, local copies, waits for them, and re-layouts  15.6 us
  transfers between devices with their start and end apart: 66, of which 27 were waited for; matrix products, arithmetic and copies ran while one was open for 36% of the time, Pallas kernels for 5%

profile of v1, /device:TPU:0, one launch (start us, length us, event | category | flops | bytes accessed | tf_op | source)
XLA Modules:
  0.0 443.1 jit_solution(8514165821577918925)
XLA Ops:
  4.9 6.1 %concatenate.32 = bf16[288]{0:T(512)(128)(2,1)S(1)} concatenate(bf16[24]{0:T(256)(128)(2,1)} %param.22, bf16[24]{0:T(256)(128)(2,1)} %param.25, bf16[24]{0:T(256)(128)(2,1)} %param.27, bf16[24]{0:T(256)(128)(2,1)} %param.28, bf16[24]{0:T(256)(128)(2,1)} %param.29, bf16[24]{0:T(256)(128)(2,1)} %param.33, bf16[24]{0:T(256)(128)(2,1)} %param.34, bf16[24]{0:T(256)(128)(2,1)} %param.35, ...), dimensions={0} | concatenate | bytes 1152 | tf_op jit(solution)/shard_map/concatenate | solution.py:272
  49.9 12.3 %collective-permute-done.10 = bf16[32,384]{1,0:T(8,128)(2,1)S(1)} collective-permute-done((bf16[32,384]{1,0:T(8,128)(2,1)S(1)}, bf16[32,384]{1,0:T(8,128)(2,1)S(1)}, u32[]{:S(2)}, u32[]{:S(2)}) %collective-permute-start.10) | collective-permute-done | bytes 24608 | tf_op jit(solution)/shard_map/ppermute | solution.py:172
  78.6 3.6 collective-permute-done.24
  88.0 4.7 %collective-permute-done.14 = bf16[2,2,2,48,384]{4,3,2,1,0:T(8,128)(2,1)S(1)} collective-permute-done((bf16[2,2,2,48,384]{4,3,2,1,0:T(8,128)(2,1)S(1)}, bf16[2,2,2,48,384]{4,3,2,1,0:T(8,128)(2,1)S(1)}, u32[]{:S(2)}, u32[]{:S(2)}) %collective-permute-start.14) | collective-permute-done | bytes 294944 | tf_op jit(solution)/shard_map/ppermute | solution.py:172
  94.1 4.8 %collective-permute-done.20 = bf16[2,2,2,48,384]{4,3,2,1,0:T(8,128)(2,1)S(1)} collective-permute-done((bf16[2,2,2,48,384]{4,3,2,1,0:T(8,128)(2,1)S(1)}, bf16[2,2,2,48,384]{4,3,2,1,0:T(8,128)(2,1)S(1)}, u32[]{:S(2)}, u32[]{:S(2)}) %collective-permute-start.20) | collective-permute-done | bytes 294944 | tf_op jit(solution)/shard_map/ppermute | solution.py:172
  104.0 6.4 %collective-permute-done.5 = bf16[2,2,2,48,768]{4,3,2,1,0:T(8,128)(2,1)S(1)} collective-permute-done((bf16[2,2,2,48,768]{4,3,2,1,0:T(8,128)(2,1)S(1)}, bf16[2,2,2,48,768]{4,3,2,1,0:T(8,128)(2,1)S(1)}, u32[]{:S(2)}, u32[]{:S(2)}) %collective-permute-start.5) | collective-permute-done | bytes 589856 | tf_op jit(solution)/shard_map/ppermute | solution.py:172
  112.6 9.4 %attend.1 = (bf16[1024,384]{1,0:T(8,128)(2,1)S(1)}, f32[2,3,2,512]{3,2,1,0:T(2,128)S(1)}) custom-call(s32[2]{0:T(128)S(1)} %copy-done, bf16[1024,768]{1,0:T(8,128)(2,1)S(1)} %add_convert_fusion.2.q_ref.k_ref, bf16[1024,768]{1,0:T(8,128)(2,1)S(1)} %add_convert_fusion.2.q_ref.k_ref, bf16[1024,384]{1,0:T(8,128)(2,1)S(1)} %add_convert_fusion.4.v_ref), custom_call_target="tpu_custom_call" | custom-call | flops 805306368 | bytes 3145728 | tf_op jit(solution)/shard_map/attend/pallas_call | solution.py:114
  150.6 3.8 copy.112
  161.9 3.7 copy.109
  167.9 3.8 bitcast_select_fusion.1
  178.2 3.5 fusion.25
  185.0 3.3 broadcast_select_fusion
  193.2 5.1 %multiply_convert_fusion = (bf16[512,1536]{1,0:T(8,128)(2,1)S(1)}, f32[512,1536]{1,0:T(8,128)}) fusion(f32[1536]{0:T(1024)S(1)} %get-tuple-element.37, bf16[512,768]{1,0:T(8,128)(2,1)S(1)} %get-tuple-element.47, bf16[768,1536]{1,0:T(8,128)(2,1)} %collective-permute-done.27), kind=kOutput, calls=%fused_computation.29 | convolution fusion | flops 1212678144 | bytes 7870464 | tf_op jit(solution)/shard_map/dot_general | solution.py:19
  206.9 3.7 copy.116
  211.9 3.4 reshape.1686
  215.4 3.7 copy.115
  236.4 3.9 convert_reduce_fusion.1
  240.3 4.8 %fusion.98 = f32[512,768]{1,0:T(8,128)} fusion(bf16[512,1536]{1,0:T(8,128)(2,1)S(1)} %get-tuple-element.41, bf16[768,1536]{1,0:T(8,128)(2,1)} %bitcast_select_fusion.1), kind=kOutput, calls=%fused_computation.311 | convolution fusion | flops 1207959552 | bytes 5505024 | tf_op jit(solution)/shard_map/dot_general | solution.py:27
  251.2 6.4 %multiply_reduce_fusion.1 = (f32[768]{0:T(1024)S(1)}, f32[512]{0:T(512)S(1)}, f32[512]{0:T(512)S(1)}, f32[768]{0:T(1024)S(1)}, f32[512,768]{1,0:T(8,128)S(1)}) fusion(f32[512,768]{1,0:T(8,128)} %get-tuple-element.48, f32[768]{0:T(1024)S(1)} %reshape.1647, f32[512,768]{1,0:T(8,128)} %fusion.98, f32[512]{0:T(512)S(1)} %bitcast.467, f32[512]{0:T(512)S(1)} %bitcast.471, ...), kind=kOutput, calls=%fused_computation.61 | convolution fusion | flops 1217000960 | bytes 12616448 | tf_op jit(solution)/shard_map/dot_general | solution.py:27
  278.7 4.5 %convolution_convert_fusion.2 = bf16[768,1536]{1,0:T(8,128)(2,1)} fusion(bf16[512,768]{1,0:T(8,128)(2,1)} %copy-done.52, bf16[512,1536]{1,0:T(8,128)(2,1)} %get-tuple-element.52), kind=kOutput, calls=%fused_computation.7 | convolution fusion | flops 1209139200 | bytes 4718592 | tf_op jit(solution)/shard_map/dot_general | solution.py:23
  284.9 13.1 %attend_back.1 = (bf16[1024,384]{1,0:T(8,128)(2,1)S(1)}, bf16[1024,384]{1,0:T(8,128)(2,1)S(1)}, bf16[1024,384]{1,0:T(8,128)(2,1)S(1)}) custom-call(s32[2]{0:T(128)S(1)} %copy-done, bf16[1024,768]{1,0:T(8,128)(2,1)S(1)} %add_convert_fusion.2.q_ref.k_ref, bf16[1024,768]{1,0:T(8,128)(2,1)S(1)} %add_convert_fusion.2.q_ref.k_ref, ...), custom_call_target="tpu_custom_call" | custom-call | flops 2013265920 | bytes 5505024 | tf_op jit(solution)/shard_map/attend_back/pallas_call | solution.py:142
  310.2 3.9 add_add_fusion
  340.0 8.3 %collective-permute-done.41 = bf16[2,2,48,384]{3,2,1,0:T(8,128)(2,1)S(1)} collective-permute-done((bf16[2,2,48,384]{3,2,1,0:T(8,128)(2,1)S(1)}, bf16[2,2,48,384]{3,2,1,0:T(8,128)(2,1)S(1)}, u32[]{:S(2)}, u32[]{:S(2)}) %collective-permute-start.41) | collective-permute-done | bytes 147488 | tf_op jit(solution)/shard_map/ppermute | solution.py:172
  349.9 5.1 %collective-permute-done.45 = bf16[2,2,2,48,384]{4,3,2,1,0:T(8,128)(2,1)S(1)} collective-permute-done((bf16[2,2,2,48,384]{4,3,2,1,0:T(8,128)(2,1)S(1)}, bf16[2,2,2,48,384]{4,3,2,1,0:T(8,128)(2,1)S(1)}, u32[]{:S(2)}, u32[]{:S(2)}) %collective-permute-start.45) | collective-permute-done | bytes 294944 | tf_op jit(solution)/shard_map/ppermute | solution.py:172
  355.2 4.1 collective-permute-done.42
  359.8 4.5 %collective-permute-done.43 = bf16[48,384]{1,0:T(8,128)(2,1)S(1)} collective-permute-done((bf16[48,384]{1,0:T(8,128)(2,1)S(1)}, bf16[48,384]{1,0:T(8,128)(2,1)S(1)}, u32[]{:S(2)}, u32[]{:S(2)}) %collective-permute-start.43) | collective-permute-done | bytes 36896 | tf_op jit(solution)/shard_map/ppermute | solution.py:172
  374.4 3.5 add_convert_fusion
  385.6 3.2 collective-permute-done.38
  391.5 11.1 %collective-permute-done.61 = bf16[2,2,2,192,384]{4,3,2,1,0:T(8,128)(2,1)S(1)} collective-permute-done((bf16[2,2,2,192,384]{4,3,2,1,0:T(8,128)(2,1)S(1)}, bf16[2,2,2,192,384]{4,3,2,1,0:T(8,128)(2,1)S(1)}, u32[]{:S(2)}, u32[]{:S(2)}) %collective-permute-start.61) | collective-permute-done | bytes 1179680 | tf_op jit(solution)/shard_map/ppermute | solution.py:172
  408.9 5.6 %collective-permute-done.62 = bf16[2,2,192,384]{3,2,1,0:T(8,128)(2,1)S(1)} collective-permute-done((bf16[2,2,192,384]{3,2,1,0:T(8,128)(2,1)S(1)}, bf16[2,2,192,384]{3,2,1,0:T(8,128)(2,1)S(1)}, u32[]{:S(2)}, u32[]{:S(2)}) %collective-permute-start.62) | collective-permute-done | bytes 589856 | tf_op jit(solution)/shard_map/ppermute | solution.py:172
  419.4 4.7 %collective-permute-done.63 = bf16[2,192,384]{2,1,0:T(8,128)(2,1)S(1)} collective-permute-done((bf16[2,192,384]{2,1,0:T(8,128)(2,1)S(1)}, bf16[2,192,384]{2,1,0:T(8,128)(2,1)S(1)}, u32[]{:S(2)}, u32[]{:S(2)}) %collective-permute-start.63) | collective-permute-done | bytes 294944 | tf_op jit(solution)/shard_map/ppermute | solution.py:172
  432.2 3.8 collective-permute-done.53
  (558 shorter events, 268.2 us)
Async XLA Ops:
  4.3 21.6 %collective-permute-start.1 = (bf16[24,1152]{1,0:T(8,128)(2,1)S(1)}, bf16[24,1152]{1,0:T(8,128)(2,1)S(1)}, u32[]{:S(2)}, u32[]{:S(2)}) collective-permute-start(bf16[24,1152]{1,0:T(8,128)(2,1)S(1)} %pad_maximum_fusion.8), channel_id=1, source_target_pairs={{0,1},{1,0},{2,3},{3,2},{4,5},{5,4},{6,7},{7,6},{8,9},{9,8},{10,11... | collective-permute-start | bytes 165896 | tf_op jit(solution)/shard_map/ppermute | solution.py:175
  4.8 18.3 %collective-permute-start.16 = (bf16[24,384]{1,0:T(8,128)(2,1)S(1)}, bf16[24,384]{1,0:T(8,128)(2,1)S(1)}, u32[]{:S(2)}, u32[]{:S(2)}) collective-permute-start(bf16[24,384]{1,0:T(8,128)(2,1)S(1)} %bitcast.459), channel_id=1, source_target_pairs={{0,1},{1,0},{2,3},{3,2},{4,5},{5,4},{6,7},{7,6},{8,9},{9,8},{10,11... | collective-permute-start | bytes 55304 | tf_op jit(solution)/shard_map/ppermute | solution.py:175
  13.5 26.7 %collective-permute-start.22 = (bf16[24,1536]{1,0:T(8,128)(2,1)}, bf16[24,1536]{1,0:T(8,128)(2,1)}, u32[]{:S(2)}, u32[]{:S(2)}) collective-permute-start(bf16[24,1536]{1,0:T(8,128)(2,1)} %bitcast.384), channel_id=1, source_target_pairs={{0,1},{1,0},{2,3},{3,2},{4,5},{5,4},{6,7},{7,6},{8,9},{9,8},{10,11... | collective-permute-start | bytes 221192 | tf_op jit(solution)/shard_map/ppermute | solution.py:175
  14.6 26.7 %collective-permute-start.28 = (bf16[96,384]{1,0:T(8,128)(2,1)}, bf16[96,384]{1,0:T(8,128)(2,1)}, u32[]{:S(2)}, u32[]{:S(2)}) collective-permute-start(bf16[96,384]{1,0:T(8,128)(2,1)} %bitcast.382), channel_id=1, source_target_pairs={{0,1},{1,0},{2,3},{3,2},{4,5},{5,4},{6,7},{7,6},{8,9},{9,8},{10,11... | collective-permute-start | bytes 221192 | tf_op jit(solution)/shard_map/ppermute | solution.py:175
  23.2 22.9 %collective-permute-start.17 = (bf16[48,384]{1,0:T(8,128)(2,1)S(1)}, bf16[48,384]{1,0:T(8,128)(2,1)S(1)}, u32[]{:S(2)}, u32[]{:S(2)}) collective-permute-start(bf16[48,384]{1,0:T(8,128)(2,1)S(1)} %bitcast_select_fusion.10), channel_id=1, source_target_pairs={{0,16},{2,18},{4,20},{6,22},{8,24},{10,26},{12,28},{14,30},{16,0},... | collective-permute-start | bytes 110600 | tf_op jit(solution)/shard_map/ppermute | solution.py:172
  26.0 22.8 %collective-permute-start.11 = (bf16[48,384]{1,0:T(8,128)(2,1)S(1)}, bf16[48,384]{1,0:T(8,128)(2,1)}, u32[]{:S(2)}, u32[]{:S(2)}) collective-permute-start(bf16[48,384]{1,0:T(8,128)(2,1)S(1)} %slice.146), channel_id=1, source_target_pairs={{0,16},{2,18},{4,20},{6,22},{8,24},{10,26},{12,28},{14,30},{16,0},... | collective-permute-start | bytes 110600 | tf_op jit(solution)/shard_map/ppermute | solution.py:172
  26.4 18.5 %collective-permute-start.9 = (bf16[32,384]{1,0:T(8,128)(2,1)S(1)}, bf16[32,384]{1,0:T(8,128)(2,1)}, u32[]{:S(2)}, u32[]{:S(2)}) collective-permute-start(bf16[32,384]{1,0:T(8,128)(2,1)S(1)} %add.462), channel_id=1, source_target_pairs={{0,8},{2,10},{4,12},{6,14},{8,0},{10,2},{12,4},{14,6},{16,24},{18,... | collective-permute-start | bytes 73736 | tf_op jit(solution)/shard_map/ppermute | solution.py:172
  40.2 61.2 %collective-permute-start = (bf16[2,256,768]{2,1,0:T(8,128)(2,1)S(1)}, bf16[2,256,768]{2,1,0:T(8,128)(2,1)S(1)}, u32[]{:S(2)}, u32[]{:S(2)}) collective-permute-start(bf16[2,256,768]{2,1,0:T(8,128)(2,1)S(1)} %copy-done.5), channel_id=1, source_target_pairs={{0,1},{1,0},{2,3},{3,2},{4,5},{5,4},{6,7},{7,6},{8,9},{9,8},{10,11... | collective-permute-start | bytes 2359304 | tf_op jit(solution)/shard_map/ppermute | solution.py:175
  41.3 23.1 %collective-permute-start.2 = (bf16[48,768]{1,0:T(8,128)(2,1)S(1)}, bf16[48,768]{1,0:T(8,128)(2,1)S(1)}, u32[]{:S(2)}, u32[]{:S(2)}) collective-permute-start(bf16[48,768]{1,0:T(8,128)(2,1)S(1)} %slice.144), channel_id=1, source_target_pairs={{0,16},{2,18},{4,20},{6,22},{8,24},{10,26},{12,28},{14,30},{16,0},... | collective-permute-start | bytes 221192 | tf_op jit(solution)/shard_map/ppermute | solution.py:172
  44.9 25.9 %collective-permute-start.23 = (bf16[48,1536]{1,0:T(8,128)(2,1)S(1)}, bf16[48,1536]{1,0:T(8,128)(2,1)S(1)}, u32[]{:S(2)}, u32[]{:S(2)}) collective-permute-start(bf16[48,1536]{1,0:T(8,128)(2,1)S(1)} %bitcast_select_fusion.8), channel_id=1, source_target_pairs={{0,16},{2,18},{4,20},{6,22},{8,24},{10,26},{12,28},{14,30},{16,0},... | collective-permute-start | bytes 442376 | tf_op jit(solution)/shard_map/ppermute | solution.py:172
  46.1 26.1 %collective-permute-start.29 = (bf16[192,384]{1,0:T(8,128)(2,1)S(1)}, bf16[192,384]{1,0:T(8,128)(2,1)S(1)}, u32[]{:S(2)}, u32[]{:S(2)}) collective-permute-start(bf16[192,384]{1,0:T(8,128)(2,1)S(1)} %bitcast_select_fusion.7), channel_id=1, source_target_pairs={{0,16},{2,18},{4,20},{6,22},{8,24},{10,26},{12,28},{14,30},{16,0},... | collective-permute-start | bytes 442376 | tf_op jit(solution)/shard_map/ppermute | solution.py:172
  48.7 13.5 %collective-permute-start.10 = (bf16[32,384]{1,0:T(8,128)(2,1)S(1)}, bf16[32,384]{1,0:T(8,128)(2,1)S(1)}, u32[]{:S(2)}, u32[]{:S(2)}) collective-permute-start(bf16[32,384]{1,0:T(8,128)(2,1)S(1)} %add.463), channel_id=1, source_target_pairs={{0,16},{2,18},{4,20},{6,22},{8,24},{10,26},{12,28},{14,30},{16,0},... | collective-permute-start | bytes 73736 | tf_op jit(solution)/shard_map/ppermute | solution.py:172
  77.0 15.6 %collective-permute-start.14 = (bf16[2,2,2,48,384]{4,3,2,1,0:T(8,128)(2,1)S(1)}, bf16[2,2,2,48,384]{4,3,2,1,0:T(8,128)(2,1)S(1)}, u32[]{:S(2)}, u32[]{:S(2)}) collective-permute-start(bf16[2,2,2,48,384]{4,3,2,1,0:T(8,128)(2,1)S(1)} %get-tuple-element.121), channel_id=1, source_target_pairs={{0,4},{2,6},{4,0},{6,2},{8,12},{10,14},{12,8},{14,10},{16,20},{18,... | collective-permute-start | bytes 884744 | tf_op jit(solution)/shard_map/ppermute | solution.py:172
  82.3 16.7 %collective-permute-start.20 = (bf16[2,2,2,48,384]{4,3,2,1,0:T(8,128)(2,1)S(1)}, bf16[2,2,2,48,384]{4,3,2,1,0:T(8,128)(2,1)S(1)}, u32[]{:S(2)}, u32[]{:S(2)}) collective-permute-start(bf16[2,2,2,48,384]{4,3,2,1,0:T(8,128)(2,1)S(1)} %get-tuple-element.120), channel_id=1, source_target_pairs={{0,4},{2,6},{4,0},{6,2},{8,12},{10,14},{12,8},{14,10},{16,20},{18,... | collective-permute-start | bytes 884744 | tf_op jit(solution)/shard_map/ppermute | solution.py:172
  85.4 37.5 %collective-permute-start.25 = (bf16[2,2,48,1536]{3,2,1,0:T(8,128)(2,1)S(1)}, bf16[2,2,48,1536]{3,2,1,0:T(8,128)(2,1)S(1)}, u32[]{:S(2)}, u32[]{:S(2)}) collective-permute-start(bf16[2,2,48,1536]{3,2,1,0:T(8,128)(2,1)S(1)} %broadcast_select_fusion.9), channel_id=1, source_target_pairs={{0,4},{2,6},{4,0},{6,2},{8,12},{10,14},{12,8},{14,10},{16,20},{18,... | collective-permute-start | bytes 1769480 | tf_op jit(solution)/shard_map/ppermute | solution.py:172
  86.3 39.3 %collective-permute-start.31 = (bf16[2,2,192,384]{3,2,1,0:T(8,128)(2,1)S(1)}, bf16[2,2,192,384]{3,2,1,0:T(8,128)(2,1)S(1)}, u32[]{:S(2)}, u32[]{:S(2)}) collective-permute-start(bf16[2,2,192,384]{3,2,1,0:T(8,128)(2,1)S(1)} %broadcast_select_fusion.8), channel_id=1, source_target_pairs={{0,2},{2,0},{4,6},{6,4},{8,10},{10,8},{12,14},{14,12},{16,18},{18,... | collective-permute-start | bytes 1769480 | tf_op jit(solution)/shard_map/ppermute | solution.py:172
  92.7 17.7 %collective-permute-start.5 = (bf16[2,2,2,48,768]{4,3,2,1,0:T(8,128)(2,1)S(1)}, bf16[2,2,2,48,768]{4,3,2,1,0:T(8,128)(2,1)S(1)}, u32[]{:S(2)}, u32[]{:S(2)}) collective-permute-start(bf16[2,2,2,48,768]{4,3,2,1,0:T(8,128)(2,1)S(1)} %broadcast_select_fusion.12), channel_id=1, source_target_pairs={{0,2},{2,0},{4,6},{6,4},{8,10},{10,8},{12,14},{14,12},{16,18},{18,... | collective-permute-start | bytes 1769480 | tf_op jit(solution)/shard_map/ppermute | solution.py:172
  100.3 42.9 %collective-permute-start.21 = (bf16[768,384]{1,0:T(8,128)(2,1)}, bf16[768,384]{1,0:T(8,128)(2,1)}, u32[]{:S(2)}, u32[]{:S(2)}) collective-permute-start(bf16[768,384]{1,0:T(8,128)(2,1)} %get-tuple-element.115), channel_id=1, source_target_pairs={{0,1},{1,0},{2,3},{3,2},{4,5},{5,4},{6,7},{7,6},{8,9},{9,8},{10,11... | collective-permute-start | bytes 1769480 | tf_op jit(solution)/shard_map/ppermute | solution.py:175
  122.9 14.1 %collective-permute-start.15 = (bf16[2,256,384]{2,1,0:T(8,128)(2,1)}, bf16[2,256,384]{2,1,0:T(8,128)(2,1)}, u32[]{:S(2)}, u32[]{:S(2)}) collective-permute-start(bf16[2,256,384]{2,1,0:T(8,128)(2,1)} %get-tuple-element.63), channel_id=1, source_target_pairs={{0,1},{1,0},{2,3},{3,2},{4,5},{5,4},{6,7},{7,6},{8,9},{9,8},{10,11... | collective-permute-start | bytes 1179656 | tf_op jit(solution)/shard_map/ppermute | solution.py:175
  124.1 43.8 %collective-permute-start.26 = (bf16[2,2,2,48,1536]{4,3,2,1,0:T(8,128)(2,1)}, bf16[2,2,2,48,1536]{4,3,2,1,0:T(8,128)(2,1)}, u32[]{:S(2)}, u32[]{:S(2)}) collective-permute-start(bf16[2,2,2,48,1536]{4,3,2,1,0:T(8,128)(2,1)} %broadcast_select_fusion.4), channel_id=1, source_target_pairs={{0,2},{2,0},{4,6},{6,4},{8,10},{10,8},{12,14},{14,12},{16,18},{18,... | collective-permute-start | bytes 3538952 | tf_op jit(solution)/shard_map/ppermute | solution.py:172
  126.9 54.8 %collective-permute-start.32 = (bf16[2,2,2,192,384]{4,3,2,1,0:T(8,128)(2,1)}, bf16[2,2,2,192,384]{4,3,2,1,0:T(8,128)(2,1)}, u32[]{:S(2)}, u32[]{:S(2)}) collective-permute-start(bf16[2,2,2,192,384]{4,3,2,1,0:T(8,128)(2,1)} %broadcast_select_fusion.3), channel_id=1, source_target_pairs={{0,4},{2,6},{4,0},{6,2},{8,12},{10,14},{12,8},{14,10},{16,20},{18,... | collective-permute-start | bytes 3538952 | tf_op jit(solution)/shard_map/ppermute | solution.py:172
  171.7 21.5 %collective-permute-start.27 = (bf16[768,1536]{1,0:T(8,128)(2,1)}, bf16[768,1536]{1,0:T(8,128)(2,1)}, u32[]{:S(2)}, u32[]{:S(2)}) collective-permute-start(bf16[768,1536]{1,0:T(8,128)(2,1)} %bitcast_select_fusion.1), channel_id=1, source_target_pairs={{0,1},{1,0},{2,3},{3,2},{4,5},{5,4},{6,7},{7,6},{8,9},{9,8},{10,11... | collective-permute-start | bytes 7077896 | tf_op jit(solution)/shard_map/ppermute | solution.py:175
  184.2 15.6 %collective-permute-start.33 = (bf16[3072,384]{1,0:T(8,128)(2,1)S(1)}, bf16[3072,384]{1,0:T(8,128)(2,1)S(1)}, u32[]{:S(2)}, u32[]{:S(2)}) collective-permute-start(bf16[3072,384]{1,0:T(8,128)(2,1)S(1)} %bitcast_select_fusion), channel_id=1, source_target_pairs={{0,1},{1,0},{2,3},{3,2},{4,5},{5,4},{6,7},{7,6},{8,9},{9,8},{10,11... | collective-permute-start | bytes 7077896 | tf_op jit(solution)/shard_map/ppermute | solution.py:175
  277.9 96.5 %collective-permute-start.60 = (bf16[3072,384]{1,0:T(8,128)(2,1)}, bf16[3072,384]{1,0:T(8,128)(2,1)}, u32[]{:S(2)}, u32[]{:S(2)}) collective-permute-start(bf16[3072,384]{1,0:T(8,128)(2,1)} %pad_maximum_fusion.2), channel_id=1, source_target_pairs={{0,1},{1,0},{2,3},{3,2},{4,5},{5,4},{6,7},{7,6},{8,9},{9,8},{10,11... | collective-permute-start | bytes 7077896 | tf_op jit(solution)/shard_map/ppermute | solution.py:175
  278.6 58.1 %collective-permute-start.44 = (bf16[768,384]{1,0:T(8,128)(2,1)}, bf16[768,384]{1,0:T(8,128)(2,1)}, u32[]{:S(2)}, u32[]{:S(2)}) collective-permute-start(bf16[768,384]{1,0:T(8,128)(2,1)} %convolution_convert_fusion.7), channel_id=1, source_target_pairs={{0,1},{1,0},{2,3},{3,2},{4,5},{5,4},{6,7},{7,6},{8,9},{9,8},{10,11... | collective-permute-start | bytes 1769480 | tf_op jit(solution)/shard_map/ppermute | solution.py:175
  283.2 96.5 %collective-permute-start.49 = (bf16[768,1536]{1,0:T(8,128)(2,1)}, bf16[768,1536]{1,0:T(8,128)(2,1)}, u32[]{:S(2)}, u32[]{:S(2)}) collective-permute-start(bf16[768,1536]{1,0:T(8,128)(2,1)} %convolution_convert_fusion.2), channel_id=1, source_target_pairs={{0,1},{1,0},{2,3},{3,2},{4,5},{5,4},{6,7},{7,6},{8,9},{9,8},{10,11... | collective-permute-start | bytes 7077896 | tf_op jit(solution)/shard_map/ppermute | solution.py:175
  332.3 32.6 %collective-permute-start.36 = (bf16[2,2,2,48,768]{4,3,2,1,0:T(8,128)(2,1)}, bf16[2,2,2,48,768]{4,3,2,1,0:T(8,128)(2,1)}, u32[]{:S(2)}, u32[]{:S(2)}) collective-permute-start(bf16[2,2,2,48,768]{4,3,2,1,0:T(8,128)(2,1)} %dynamic-slice_bitcast_fusion.4), channel_id=1, source_target_pairs={{0,2},{2,0},{4,6},{6,4},{8,10},{10,8},{12,14},{14,12},{16,18},{18,... | collective-permute-start | bytes 1769480 | tf_op jit(solution)/shard_map/ppermute | solution.py:172
  335.6 100.6 %collective-permute-start.35 = (bf16[2,256,768]{2,1,0:T(8,128)(2,1)}, bf16[2,256,768]{2,1,0:T(8,128)(2,1)S(1)}, u32[]{:S(2)}, u32[]{:S(2)}) collective-permute-start(bf16[2,256,768]{2,1,0:T(8,128)(2,1)} %fusion.31), channel_id=1, source_target_pairs={{0,1},{1,0},{2,3},{3,2},{4,5},{5,4},{6,7},{7,6},{8,9},{9,8},{10,11... | collective-permute-start | bytes 2359304 | tf_op jit(solution)/shard_map/ppermute | solution.py:175
  369.8 13.8 %collective-permute-start.37 = (bf16[2,2,48,768]{3,2,1,0:T(8,128)(2,1)S(1)}, bf16[2,2,48,768]{3,2,1,0:T(8,128)(2,1)S(1)}, u32[]{:S(2)}, u32[]{:S(2)}) collective-permute-start(bf16[2,2,48,768]{3,2,1,0:T(8,128)(2,1)S(1)} %dynamic-slice_bitcast_fusion.12), channel_id=1, source_target_pairs={{0,4},{2,6},{4,0},{6,2},{8,12},{10,14},{12,8},{14,10},{16,20},{18,... | collective-permute-start | bytes 884744 | tf_op jit(solution)/shard_map/ppermute | solution.py:172
  378.1 24.5 %collective-permute-start.61 = (bf16[2,2,2,192,384]{4,3,2,1,0:T(8,128)(2,1)S(1)}, bf16[2,2,2,192,384]{4,3,2,1,0:T(8,128)(2,1)S(1)}, u32[]{:S(2)}, u32[]{:S(2)}) collective-permute-start(bf16[2,2,2,192,384]{4,3,2,1,0:T(8,128)(2,1)S(1)} %dynamic-slice_bitcast_fusion), channel_id=1, source_target_pairs={{0,4},{2,6},{4,0},{6,2},{8,12},{10,14},{12,8},{14,10},{16,20},{18,... | collective-permute-start | bytes 3538952 | tf_op jit(solution)/shard_map/ppermute | solution.py:172
  382.9 23.9 %collective-permute-start.50 = (bf16[2,2,2,48,1536]{4,3,2,1,0:T(8,128)(2,1)S(1)}, bf16[2,2,2,48,1536]{4,3,2,1,0:T(8,128)(2,1)S(1)}, u32[]{:S(2)}, u32[]{:S(2)}) collective-permute-start(bf16[2,2,2,48,1536]{4,3,2,1,0:T(8,128)(2,1)S(1)} %dynamic-slice_bitcast_fusion.1), channel_id=1, source_target_pairs={{0,2},{2,0},{4,6},{6,4},{8,10},{10,8},{12,14},{14,12},{16,18},{18,... | collective-permute-start | bytes 3538952 | tf_op jit(solution)/shard_map/ppermute | solution.py:172
  388.9 20.0 %collective-permute-start.39 = (bf16[48,768]{1,0:T(8,128)(2,1)S(1)}, bf16[48,768]{1,0:T(8,128)(2,1)S(1)}, u32[]{:S(2)}, u32[]{:S(2)}) collective-permute-start(bf16[48,768]{1,0:T(8,128)(2,1)S(1)} %dynamic-slice_bitcast_fusion.22), channel_id=1, source_target_pairs={{0,16},{2,18},{4,20},{6,22},{8,24},{10,26},{12,28},{14,30},{16,0},... | collective-permute-start | bytes 221192 | tf_op jit(solution)/shard_map/ppermute | solution.py:172
  (119 other events, 720.5 us)
